TPU v7x, 32 devices: a whole 2x2x4 slice. The times are simulated.
32 devices in a mesh: dp: 8 (over z, core), tensor: 4 (over y, x).
Axes of the slice: x: 2, y: 2, z: 4, core: 2. Of those that a mesh axis runs over, the one named last changes fastest.
Arguments:
- hidden_in: bfloat16 [2048, 8192], P(('dp', 'tensor')), may hold values from -6 to 6
- out_grad: bfloat16 [2048, 8192], P(('dp', 'tensor')), may hold values from -0.29882812 to 0.29882812
- seq_lengths: int32 [8, 8], P('dp'), may hold values from 1 to 128, 256 in all within a row
- seq_adapter: int32 [8, 8], P('dp'), may hold values from 0 to 15
- query_weight: bfloat16 [8192, 4096], P(None, 'tensor'), may hold values from -0.0625 to 0.0625
- key_value_weight: bfloat16 [2, 8192, 1024], P(None, None, 'tensor'), may hold values from -0.0625 to 0.0625
- output_weight: bfloat16 [4096, 8192], P('tensor'), may hold values from -0.09375 to 0.09375
- a_in: bfloat16 [16, 48, 8192], P('dp', None, 'tensor'), may hold values from -0.0625 to 0.0625
- b_query: bfloat16 [16, 16, 4096], P('dp', None, 'tensor'), may hold values from -0.375 to 0.375
- b_key_value: bfloat16 [16, 2, 16, 1024], P('dp', None, None, 'tensor'), may hold values from -0.375 to 0.375
- output_down_factor: bfloat16 [16, 16, 4096], P('dp', None, 'tensor'), may hold values from -0.09375 to 0.09375
- output_up_factor: bfloat16 [16, 16, 8192], P('dp', 'tensor'), may hold values from -0.375 to 0.375
Outputs:
- attn_out: bfloat16 [2048, 8192], P(('dp', 'tensor'))
- input_grad: bfloat16 [2048, 8192], P(('dp', 'tensor'))
- input_down_gradient: float32 [16, 48, 8192], P('dp', None, 'tensor')
- query_up_gradient: float32 [16, 16, 4096], P('dp', None, 'tensor')
- grad_b_key_value: float32 [16, 2, 16, 1024], P('dp', None, None, 'tensor')
- output_down_gradient: float32 [16, 16, 4096], P('dp', None, 'tensor')
- output_up_gradient: float32 [16, 16, 8192], P('dp', 'tensor')
All inputs are finite; a program needn't handle non-finite values.
Results may differ from a plain program's by a relative error of at most 0.015.
Values may be sent and summed in bfloat16 or wider, within the bound.
A program may use at most 192 MiB of HBM per device.

v0:
```python
import jax
import jax.numpy as jnp
from jax import lax
from jax.sharding import PartitionSpec as P

HEAD_SIZE = 128
adapter_scale = 2.0
rope_theta = 500000.0
masked_score = -1e30


def contract_trailing_axis(left, right):
    return lax.dot_general(
        left, right, (((1,), (1,)), ((), ())), preferred_element_type=jnp.float32
    )


def contract_leading_axis(left, right):
    return lax.dot_general(
        left, right, (((0,), (0,)), ((), ())), preferred_element_type=jnp.float32
    )


def token_tables(lengths, adapters, tok_total, adapter_overall_count):
    seq_ends = jnp.cumsum(lengths)
    seq_starts = seq_ends - lengths
    token_ids = jnp.arange(tok_total, dtype=jnp.int32)
    member = (
        (token_ids[:, None] >= seq_starts[None, :]) & (token_ids[:, None] < seq_ends[None, :])
    ).astype(jnp.int32)
    seq_index = jnp.sum(member * jnp.arange(lengths.shape[0], dtype=jnp.int32)[None, :], axis=1)
    position = token_ids - jnp.sum(member * seq_starts[None, :], axis=1)
    adapter_of = jnp.sum(member * adapters[None, :], axis=1)
    adapter_hot = adapter_of[:, None] == jnp.arange(adapter_overall_count, dtype=jnp.int32)[None, :]
    allowed = (seq_index[:, None] == seq_index[None, :]) & (
        token_ids[None, :] <= token_ids[:, None]
    )
    return (position, adapter_hot, allowed)


def rope_tables(position):
    half_dim = HEAD_SIZE // 2
    inverse = rope_theta ** (-(jnp.arange(half_dim, dtype=jnp.float32) * (2.0 / HEAD_SIZE)))
    angle = position.astype(jnp.float32)[:, None] * inverse[None, :]
    cosine_table = jnp.concatenate([jnp.cos(angle), jnp.cos(angle)], axis=1)
    sine_table = jnp.concatenate([jnp.sin(angle), jnp.sin(angle)], axis=1)
    return (cosine_table, sine_table)


def apply_rotation(vectors, cosine_table, sine_table):
    half_dim = HEAD_SIZE // 2
    turned = jnp.concatenate([-vectors[..., half_dim:], vectors[..., :half_dim]], axis=-1)
    return vectors * cosine_table[:, None, :] + turned * sine_table[:, None, :]


def choose_rank_rows(onehot_single, product, rank_width):
    shaped = product.reshape(product.shape[0], onehot_single.shape[1], rank_width)
    return jnp.sum(shaped * onehot_single[:, :, None], axis=1)


def expand_from_rank(onehot_halfprec, factors):
    return (onehot_halfprec[:, :, None] * factors[:, None, :]).reshape(
        factors.shape[0], onehot_halfprec.shape[1] * factors.shape[1]
    )


def attend(queries, rotated_keys, incoming_values, allowed):
    tok_total, head_count, _ = queries.shape
    group_count = rotated_keys.shape[1]
    per_group = head_count // group_count
    grouped = queries.reshape(tok_total, group_count, per_group, HEAD_SIZE)
    scores = jnp.einsum(
        "tgpe,sge->gpts", grouped, rotated_keys, preferred_element_type=jnp.float32
    ) * HEAD_SIZE ** (-0.5)
    scores = jnp.where(allowed[None, None], scores, masked_score)
    peak = jnp.max(scores, axis=-1, keepdims=True)
    expped = jnp.exp(scores - peak)
    probs = expped / jnp.sum(expped, axis=-1, keepdims=True)
    probs_bf = probs.astype(jnp.bfloat16)
    blended_output = jnp.einsum(
        "gpts,sge->tgpe", probs_bf, incoming_values, preferred_element_type=jnp.float32
    )
    return (
        blended_output.reshape(tok_total, head_count * HEAD_SIZE).astype(jnp.bfloat16),
        probs,
        probs_bf,
    )


def attend_back(queries, rotated_keys, incoming_values, probs, probs_bf, blended_gradient):
    tok_total, head_count, _ = queries.shape
    group_count = rotated_keys.shape[1]
    per_group = head_count // group_count
    incoming_gradient = blended_gradient.reshape(tok_total, group_count, per_group, HEAD_SIZE)
    grad_probs = jnp.einsum(
        "tgpe,sge->gpts", incoming_gradient, incoming_values, preferred_element_type=jnp.float32
    )
    grad_values = jnp.einsum(
        "gpts,tgpe->sge", probs_bf, incoming_gradient, preferred_element_type=jnp.float32
    )
    inner = jnp.sum(grad_probs * probs, axis=-1, keepdims=True)
    grad_scores = (probs * (grad_probs - inner) * HEAD_SIZE ** (-0.5)).astype(jnp.bfloat16)
    grouped = queries.reshape(tok_total, group_count, per_group, HEAD_SIZE)
    grad_queries = jnp.einsum(
        "gpts,sge->tgpe", grad_scores, rotated_keys, preferred_element_type=jnp.float32
    )
    grad_keys = jnp.einsum(
        "gpts,tgpe->sge", grad_scores, grouped, preferred_element_type=jnp.float32
    )
    return (grad_queries.reshape(tok_total, head_count, HEAD_SIZE), grad_keys, grad_values)


def local(
    hidden_in,
    out_grad,
    seq_lengths,
    seq_adapter,
    query_weight,
    key_value_weight,
    output_weight,
    a_in,
    b_query,
    b_key_value,
    output_down_factor,
    output_up_factor,
):
    mesh_parts = lax.axis_size("tensor")
    own_slot = lax.axis_index("tensor")
    tok_rows = hidden_in.shape[0]
    tok_total = tok_rows * mesh_parts
    full_width = hidden_in.shape[1]
    narrow_cast = full_width // mesh_parts
    adapter_rank_rows = output_down_factor.shape[1]
    rank_piece = output_up_factor.shape[1]
    query_columns = query_weight.shape[1]
    key_value_columns = key_value_weight.shape[2]
    input_down_every, query_up_every, key_value_up_every, output_down_every, b_out_all = (
        lax.all_gather(a_in, "dp", axis=0, tiled=True),
        lax.all_gather(b_query, "dp", axis=0, tiled=True),
        lax.all_gather(b_key_value, "dp", axis=0, tiled=True),
        lax.all_gather(output_down_factor, "dp", axis=0, tiled=True),
        lax.all_gather(output_up_factor, "dp", axis=0, tiled=True),
    )
    adapter_overall_count = input_down_every.shape[0]
    position, adapter_hot, allowed = token_tables(
        seq_lengths[0], seq_adapter[0], tok_total, adapter_overall_count
    )
    onehot_single = adapter_hot.astype(jnp.float32)
    onehot_halfprec = adapter_hot.astype(jnp.bfloat16)
    cosine_table, sine_table = rope_tables(position)
    input_down_flattened = input_down_every.reshape(
        adapter_overall_count * 3 * adapter_rank_rows, narrow_cast
    )
    query_up_flattened = query_up_every.reshape(
        adapter_overall_count * adapter_rank_rows, query_columns
    )
    key_up_flattened = key_value_up_every[:, 0].reshape(
        adapter_overall_count * adapter_rank_rows, key_value_columns
    )
    value_up_flattened = key_value_up_every[:, 1].reshape(
        adapter_overall_count * adapter_rank_rows, key_value_columns
    )
    output_down_flattened = output_down_every.reshape(
        adapter_overall_count * adapter_rank_rows, query_columns
    )
    output_up_flattened = b_out_all.reshape(adapter_overall_count * rank_piece, full_width)
    gathered = lax.all_gather(hidden_in, "tensor", axis=0, tiled=True)
    col_start = own_slot * narrow_cast
    local_columns = lax.dynamic_slice_in_dim(gathered, col_start, narrow_cast, 1)
    rank_partial_sum = choose_rank_rows(
        onehot_single,
        contract_trailing_axis(local_columns, input_down_flattened),
        3 * adapter_rank_rows,
    )
    input_rank_rows = lax.psum(rank_partial_sum, "tensor").astype(jnp.bfloat16)
    adapter_query_delta = expand_from_rank(onehot_halfprec, input_rank_rows[:, :adapter_rank_rows])
    adapter_key_delta = expand_from_rank(
        onehot_halfprec, input_rank_rows[:, adapter_rank_rows : 2 * adapter_rank_rows]
    )
    adapter_value_delta = expand_from_rank(
        onehot_halfprec, input_rank_rows[:, 2 * adapter_rank_rows :]
    )
    query_before_rotation = jnp.dot(
        gathered, query_weight, preferred_element_type=jnp.float32
    ) + adapter_scale * jnp.dot(
        adapter_query_delta, query_up_flattened, preferred_element_type=jnp.float32
    )
    key_before_rotation = jnp.dot(
        gathered, key_value_weight[0], preferred_element_type=jnp.float32
    ) + adapter_scale * jnp.dot(
        adapter_key_delta, key_up_flattened, preferred_element_type=jnp.float32
    )
    value_projected = jnp.dot(
        gathered, key_value_weight[1], preferred_element_type=jnp.float32
    ) + adapter_scale * jnp.dot(
        adapter_value_delta, value_up_flattened, preferred_element_type=jnp.float32
    )
    queries = apply_rotation(
        query_before_rotation.reshape(tok_total, query_columns // HEAD_SIZE, HEAD_SIZE),
        cosine_table,
        sine_table,
    ).astype(jnp.bfloat16)
    rotated_keys = apply_rotation(
        key_before_rotation.reshape(tok_total, key_value_columns // HEAD_SIZE, HEAD_SIZE),
        cosine_table,
        sine_table,
    ).astype(jnp.bfloat16)
    incoming_values = value_projected.reshape(
        tok_total, key_value_columns // HEAD_SIZE, HEAD_SIZE
    ).astype(jnp.bfloat16)
    blended_output, probs, probs_bf = attend(queries, rotated_keys, incoming_values, allowed)
    output_partial_sum = choose_rank_rows(
        onehot_single,
        contract_trailing_axis(blended_output, output_down_flattened),
        adapter_rank_rows,
    )
    output_rank_rows = lax.psum(output_partial_sum, "tensor").astype(jnp.bfloat16)
    adapter_output_delta = expand_from_rank(
        onehot_halfprec,
        lax.dynamic_slice_in_dim(output_rank_rows, own_slot * rank_piece, rank_piece, 1),
    )
    adapter_row_values = adapter_output_delta
    attn_out = lax.psum_scatter(
        (
            jnp.dot(blended_output, output_weight, preferred_element_type=jnp.float32)
            + adapter_scale
            * jnp.dot(adapter_row_values, output_up_flattened, preferred_element_type=jnp.float32)
        ).astype(jnp.bfloat16),
        "tensor",
        scatter_dimension=0,
        tiled=True,
    )
    incoming_gradient = lax.all_gather(out_grad, "tensor", axis=0, tiled=True)
    grad_part = (
        adapter_scale
        * choose_rank_rows(
            onehot_single,
            contract_trailing_axis(incoming_gradient, output_up_flattened),
            rank_piece,
        )
    ).astype(jnp.bfloat16)
    output_rank_gradient = lax.all_gather(grad_part, "tensor", axis=1, tiled=True)
    output_up_gradient = (
        adapter_scale * contract_leading_axis(adapter_output_delta, incoming_gradient)
    ).reshape(adapter_overall_count, rank_piece, full_width)
    adapter_output_gradient = expand_from_rank(onehot_halfprec, output_rank_gradient)
    blended_gradient = (
        contract_trailing_axis(incoming_gradient, output_weight)
        + jnp.dot(
            adapter_output_gradient, output_down_flattened, preferred_element_type=jnp.float32
        )
    ).astype(jnp.bfloat16)
    output_down_gradient = contract_leading_axis(adapter_output_gradient, blended_output).reshape(
        adapter_overall_count, adapter_rank_rows, query_columns
    )
    grad_queries, grad_keys, grad_values = attend_back(
        queries, rotated_keys, incoming_values, probs, probs_bf, blended_gradient
    )
    query_gradient_rows = (
        apply_rotation(grad_queries, cosine_table, -sine_table)
        .reshape(tok_total, query_columns)
        .astype(jnp.bfloat16)
    )
    key_gradient_rows = (
        apply_rotation(grad_keys, cosine_table, -sine_table)
        .reshape(tok_total, key_value_columns)
        .astype(jnp.bfloat16)
    )
    value_gradient_rows = grad_values.reshape(tok_total, key_value_columns).astype(jnp.bfloat16)
    backward_partial_sum = jnp.concatenate(
        [
            choose_rank_rows(
                onehot_single,
                contract_trailing_axis(query_gradient_rows, query_up_flattened),
                adapter_rank_rows,
            ),
            choose_rank_rows(
                onehot_single,
                contract_trailing_axis(key_gradient_rows, key_up_flattened),
                adapter_rank_rows,
            ),
            choose_rank_rows(
                onehot_single,
                contract_trailing_axis(value_gradient_rows, value_up_flattened),
                adapter_rank_rows,
            ),
        ],
        axis=1,
    )
    input_rank_gradient = (adapter_scale * lax.psum(backward_partial_sum, "tensor")).astype(
        jnp.bfloat16
    )
    query_up_gradient = (
        adapter_scale * contract_leading_axis(adapter_query_delta, query_gradient_rows)
    ).reshape(adapter_overall_count, adapter_rank_rows, query_columns)
    key_up_gradient = (
        adapter_scale * contract_leading_axis(adapter_key_delta, key_gradient_rows)
    ).reshape(adapter_overall_count, adapter_rank_rows, key_value_columns)
    value_up_gradient = (
        adapter_scale * contract_leading_axis(adapter_value_delta, value_gradient_rows)
    ).reshape(adapter_overall_count, adapter_rank_rows, key_value_columns)
    grad_b_kv = jnp.stack([key_up_gradient, value_up_gradient], axis=1)
    adapter_input_gradient = expand_from_rank(onehot_halfprec, input_rank_gradient)
    input_down_gradient = contract_leading_axis(adapter_input_gradient, local_columns).reshape(
        adapter_overall_count, 3 * adapter_rank_rows, narrow_cast
    )
    adapter_row_values = adapter_input_gradient
    heads_sum = contract_trailing_axis(query_gradient_rows, query_weight) + contract_trailing_axis(
        key_gradient_rows, key_value_weight[0]
    )
    heads_sum = heads_sum + contract_trailing_axis(value_gradient_rows, key_value_weight[1])
    adjacent_columns = jnp.dot(
        adapter_row_values, input_down_flattened, preferred_element_type=jnp.float32
    )
    placed = lax.dynamic_update_slice_in_dim(
        jnp.zeros((lax.axis_size("tensor") * tok_rows, full_width), jnp.float32),
        adjacent_columns,
        col_start,
        1,
    )
    input_grad = lax.psum_scatter(
        (heads_sum + placed).astype(jnp.bfloat16), "tensor", scatter_dimension=0, tiled=True
    )
    summed_a_in, summed_b_query, summed_b_kv, summed_a_out, summed_b_out = (
        lax.psum_scatter(input_down_gradient, "dp", scatter_dimension=0, tiled=True),
        lax.psum_scatter(query_up_gradient, "dp", scatter_dimension=0, tiled=True),
        lax.psum_scatter(grad_b_kv, "dp", scatter_dimension=0, tiled=True),
        lax.psum_scatter(output_down_gradient, "dp", scatter_dimension=0, tiled=True),
        lax.psum_scatter(output_up_gradient, "dp", scatter_dimension=0, tiled=True),
    )
    return (
        attn_out,
        input_grad,
        summed_a_in,
        summed_b_query,
        summed_b_kv,
        summed_a_out,
        summed_b_out,
    )


def solution(mesh):
    in_specs = (
        P(("dp", "tensor"), None),
        P(("dp", "tensor"), None),
        P("dp", None),
        P("dp", None),
        P(None, "tensor"),
        P(None, None, "tensor"),
        P("tensor", None),
        P("dp", None, "tensor"),
        P("dp", None, "tensor"),
        P("dp", None, None, "tensor"),
        P("dp", None, "tensor"),
        P("dp", "tensor", None),
    )
    out_specs = (
        P(("dp", "tensor"), None),
        P(("dp", "tensor"), None),
        P("dp", None, "tensor"),
        P("dp", None, "tensor"),
        P("dp", None, None, "tensor"),
        P("dp", None, "tensor"),
        P("dp", "tensor", None),
    )
    return jax.shard_map(local, mesh=mesh, in_specs=in_specs, out_specs=out_specs, check_vma=False)
```

profile of v0, /device:TPU:0, one launch (start us, length us, event | category | flops | bytes accessed | tf_op | source)
XLA Modules:
  0.0 614.8 jit_solution(17167570973509118959)
XLA Ops:
  7.2 0.7 all-gather.10.cloned.1.call-update
  8.0 0.7 all-gather.12.cloned.1.call-update
  8.7 0.7 all-gather.8.cloned.1.call-update
  10.0 0.8 reduce-window.4
  10.9 0.8 copy.119
  11.6 16.5 %all_gather.26 = bf16[16,2,16,256]{3,2,0,1:T(8,128)(2,1)S(1)} all-gather(bf16[2,2,16,256]{3,2,0,1:T(8,128)(2,1)S(1)} %copy.119), channel_id=1, replica_groups=mesh['dp'=8,'tensor'=4] {'dp'}, dimensions={0}, use_global_device_ids=true | all-gather | bytes 294912 | tf_op jit(solution)/shard_map/all_gather | solution.py:140
  28.2 0.7 fusion.88
  28.8 0.7 select_reduce_fusion
  30.0 0.7 fusion.64
  30.7 15.2 %all_gather.27 = bf16[16,16,1024]{2,1,0:T(8,128)(2,1)S(1)} all-gather(bf16[2,16,1024]{2,1,0:T(8,128)(2,1)} %param.20), channel_id=1, replica_groups=mesh['dp'=8,'tensor'=4] {'dp'}, dimensions={0}, use_global_device_ids=true | all-gather | bytes 589824 | tf_op jit(solution)/shard_map/all_gather | solution.py:139
  45.9 15.1 %all_gather.28 = bf16[16,16,1024]{2,1,0:T(8,128)(2,1)S(1)} all-gather(bf16[2,16,1024]{2,1,0:T(8,128)(2,1)S(1)} %copy-done.22), channel_id=1, replica_groups=mesh['dp'=8,'tensor'=4] {'dp'}, dimensions={0}, use_global_device_ids=true | all-gather | bytes 589824 | tf_op jit(solution)/shard_map/all_gather | solution.py:141
  61.1 28.5 %all-gather.12.cloned.1.call-done = bf16[256,8192]{1,0:T(8,128)(2,1)} async-done(((bf16[64,8192]{1,0:T(8,128)(2,1)}), bf16[256,8192]{1,0:T(8,128)(2,1)}) %all-gather.12.cloned.1.call-update) | async-done | bytes 4194320 | tf_op jit(solution)/shard_map/all_gather | solution.py:233
  89.6 3.9 fusion.36
  93.5 8.0 %all-gather = bf16[4,4,256]{2,1,0:T(4,128)(2,1)S(1)} all-gather(bf16[1,4,256]{2,1,0:T(4,128)(2,1)S(1)} %fusion.85), channel_id=1, replica_groups=mesh['dp'=8,'tensor'=4] {'tensor'}, dimensions={0}, use_global_device_ids=true | all-gather | bytes 10240 | tf_op jit(solution)/shard_map/all_gather | solution.py:242
  101.5 28.0 %all-gather.8.cloned.1.call-done = bf16[16,48,2048]{2,1,0:T(8,128)(2,1)} async-done(((bf16[2,48,2048]{2,1,0:T(8,128)(2,1)}), bf16[16,48,2048]{2,1,0:T(8,128)(2,1)}) %all-gather.8.cloned.1.call-update) | async-done | bytes 3145744 | tf_op jit(solution)/shard_map/all_gather | solution.py:138
  129.5 53.3 %all-gather.6.cloned.1.call-done = bf16[256,8192]{1,0:T(8,128)(2,1)} async-done(((bf16[64,8192]{1,0:T(8,128)(2,1)}), bf16[256,8192]{1,0:T(8,128)(2,1)}) %all-gather.6.cloned.1.call-update) | async-done | bytes 4194320 | tf_op jit(solution)/shard_map/all_gather | solution.py:167
  182.8 3.2 fusion.24
  186.1 15.7 %psum.21 = bf16[256,48]{0,1:T(8,128)(2,1)S(1)} all-reduce(f32[256,48]{0,1:T(8,128)S(1)} %fusion.24), channel_id=1, replica_groups=mesh['dp'=8,'tensor'=4] {'tensor'}, use_global_device_ids=true, to_apply=%region_3.4 | all-reduce | flops 12288 | bytes 73728 | tf_op jit(solution)/shard_map/psum | solution.py:175
  201.8 0.7 broadcast_multiply_fusion.1
  202.5 5.2 fusion.7
  208.0 0.7 slice_negate_fusion.3
  209.0 1.0 copy-done.19
  210.0 9.7 %convolution_add_fusion.4 = f32[256,1024]{1,0:T(8,128)} fusion(f32[256,1024]{1,0:T(8,128)S(1)} %fusion.22, bf16[256,8192]{1,0:T(8,128)(2,1)S(1)} %copy-done.19, bf16[8192,1024]{1,0:T(8,128)(2,1)} %param.16), kind=kOutput, calls=%fused_computation.33 | convolution fusion | flops 4295229440 | bytes 23068672 | tf_op jit(solution)/shard_map/dot_general | solution.py:183
  219.8 1.6 copy.164
  221.3 1.3 convolution_bitcast_fusion.2
  222.6 11.7 %fusion.23 = bf16[256,1024]{1,0:T(8,128)(2,1)S(1)} fusion(f32[256,1024]{1,0:T(8,128)} %convolution_bitcast_fusion.2, bf16[256,8192]{1,0:T(8,128)(2,1)} %all-gather.12.cloned.1.call-done, bf16[1024,8192]{1,0:T(8,128)(2,1)} %param.18), kind=kOutput, calls=%fused_computation.40 | convolution fusion | flops 4295491584 | bytes 22544384 | tf_op jit(solution)/shard_map/dot_general | solution.py:13
  234.7 5.2 fusion.10
  239.9 0.9 fusion.27
  240.9 1.0 fusion.40
  241.9 3.2 fusion.99
  245.1 2.2 fusion.28
  247.7 1.8 fusion.100
  249.5 4.3 convolution_bitcast_fusion.5
  253.8 4.3 fusion.51
  258.1 0.8 fusion.32
  259.1 0.9 copy.141
  260.0 1.3 fusion.29
  261.9 0.8 copy.139
  262.8 1.2 broadcast_multiply_fusion
  264.7 16.0 %all-reduce.3 = (bf16[256,16]{0,1:T(8,128)(2,1)S(1)}, f32[256,48]{0,1:T(8,128)S(1)}) all-reduce(f32[256,16]{0,1:T(8,128)S(1)} %fusion.29, f32[256,48]{0,1:T(8,128)S(1)} %pad_maximum_fusion.4), channel_id=1, replica_groups=mesh['dp'=8,'tensor'=4] {'tensor'}, use_global_device_ids=true, to_apply=%region_9.10 | all-reduce | flops 16384 | bytes 122880 | tf_op jit(solution)/shard_map/psum | solution.py:217
  280.8 3.0 convolution_multiply_fusion
  283.9 1.7 reshape.308
  285.5 1.9 pad_maximum_fusion.1
  287.5 2.4 fusion.72
  290.0 1.4 convolution_multiply_fusion.1
  291.5 1.3 fusion.2
  292.8 12.4 %fusion.3 = bf16[256,8192]{1,0:T(8,128)(2,1)} fusion(f32[256,8192]{1,0:T(8,128)S(1)} %fusion.2, bf16[256,1024]{0,1:T(8,128)(2,1)S(1)} %bitcast.233, bf16[1024,8192]{1,0:T(8,128)(2,1)} %param.18), kind=kOutput, calls=%fused_computation.7 | convolution fusion | flops 4299161600 | bytes 29884416 | tf_op jit(solution)/shard_map/dot_general | solution.py:225
  305.3 1.2 copy-done
  306.7 19.4 %fusion.101 = f32[256,8192]{1,0:T(8,128)} fusion(bf16[256,1024]{0,1:T(8,128)(2,1)S(1)} %fusion.42, bf16[8192,1024]{1,0:T(8,128)(2,1)} %param.16), kind=kOutput, calls=%fused_computation.162 | convolution fusion | flops 4294967296 | bytes 25690112 | tf_op jit(solution)/shard_map/dot_general | solution.py:13
  326.1 6.3 %convolution_add_fusion.1 = f32[256,8192]{1,0:T(8,128)S(1)} fusion(f32[256,8192]{1,0:T(8,128)} %fusion.101, bf16[256,256]{0,1:T(8,128)(2,1)S(1)} %bitcast.244, bf16[2,8192,256]{2,1,0:T(8,128)(2,1)} %param.17), kind=kOutput, calls=%fused_computation.3 | convolution fusion | flops 1075838976 | bytes 21102592 | tf_op jit(solution)/shard_map/dot_general | solution.py:13
  332.5 3.8 convolution_add_fusion
  336.3 1.2 fusion.17
  337.5 2.5 convert_element_type.128
  340.1 4.9 fusion.45
  345.0 0.6 copy-done.27
  346.9 9.6 %all-reduce.6.cloned.1.call-done = (f32[16,2,16,256]{3,2,0,1:T(8,128)}, f32[16,4,8192]{2,1,0:T(4,128)}) async-done(((f32[16,2,16,256]{3,2,0,1:T(8,128)}, f32[16,4,8192]{2,1,0:T(4,128)}), (f32[16,2,16,256]{3,2,0,1:T(8,128)}, f32[16,4,8192]{2,1,0:T(4,128)})) %all-reduce.6.cloned.1.call-update) | async-done | bytes 2621456
  356.5 0.8 constant_dynamic-slice_fusion.1
  357.4 0.6 copy.143
  358.0 1.7 constant_dynamic-slice_fusion
  359.7 30.9 %reduce-scatter.17.cloned.1.call-done = f32[2,16,1024]{2,1,0:T(8,128)} async-done(((f32[16,16,1024]{2,1,0:T(8,128)}), f32[2,16,1024]{2,1,0:T(8,128)}) %reduce-scatter.17.cloned.1.call-update) | async-done | bytes 131088 | tf_op jit(solution)/shard_map/reduce_scatter | solution.py:328
  390.6 33.5 %reduce-scatter.15.cloned.1.call-done = f32[2,16,1024]{2,1,0:T(8,128)} async-done(((f32[16,16,1024]{2,1,0:T(8,128)}), f32[2,16,1024]{2,1,0:T(8,128)}) %reduce-scatter.15.cloned.1.call-update) | async-done | bytes 131088 | tf_op jit(solution)/shard_map/reduce_scatter | solution.py:326
  424.1 54.6 %reduce-scatter.9.cloned.1.call-done = bf16[64,8192]{1,0:T(8,128)(2,1)} async-done(((bf16[256,8192]{1,0:T(8,128)(2,1)}), bf16[64,8192]{1,0:T(8,128)(2,1)}) %reduce-scatter.9.cloned.1.call-update) | async-done | bytes 1048592 | tf_op jit(solution)/shard_map/reduce_scatter | solution.py:223
  478.7 56.5 %reduce-scatter.11.cloned.1.call-done = bf16[64,8192]{1,0:T(8,128)(2,1)} async-done(((bf16[256,8192]{1,0:T(8,128)(2,1)}), bf16[64,8192]{1,0:T(8,128)(2,1)}) %reduce-scatter.11.cloned.1.call-update) | async-done | bytes 1048592 | tf_op jit(solution)/shard_map/reduce_scatter | solution.py:321
  535.2 72.6 %reduce-scatter.13.cloned.1.call-done = f32[2,48,2048]{2,1,0:T(8,128)} async-done(((f32[16,48,2048]{2,1,0:T(8,128)}), f32[2,48,2048]{2,1,0:T(8,128)}) %reduce-scatter.13.cloned.1.call-update) | async-done | bytes 786448 | tf_op jit(solution)/shard_map/reduce_scatter | solution.py:325
  (106 shorter events, 5.1 us)
Async XLA Ops:
  7.2 38.7 %copy-start.22 = (bf16[2,16,1024]{2,1,0:T(8,128)(2,1)S(1)}, bf16[2,16,1024]{2,1,0:T(8,128)(2,1)}, u32[]{:S(2)}) copy-start(bf16[2,16,1024]{2,1,0:T(8,128)(2,1)} %param.22) | copy-start | bytes 196612
  7.2 53.9 %all-gather.10.cloned.1.call-start = ((), (), s32[]{:S(2)}) async-start(), calls=%async_computation.7 | async-start | bytes 1179648 | tf_op jit(solution)/shard_map/all_gather | solution.py:142
  7.9 81.7 %all-gather.12.cloned.1.call-start = ((), (), s32[]{:S(2)}) async-start(), calls=%async_computation.9 | async-start | bytes 5242880 | tf_op jit(solution)/shard_map/all_gather | solution.py:233
  8.7 120.9 %all-gather.8.cloned.1.call-start = ((), (), s32[]{:S(2)}) async-start(), calls=%async_computation.6 | async-start | bytes 3538944 | tf_op jit(solution)/shard_map/all_gather | solution.py:138
  9.4 173.4 %all-gather.6.cloned.1.call-start = ((), (), s32[]{:S(2)}) async-start(), calls=%async_computation.5 | async-start | bytes 5242880 | tf_op jit(solution)/shard_map/all_gather | solution.py:167
  10.0 346.5 %all-reduce.6.cloned.1.call-start = ((), (), s32[]{:S(2)}) async-start(), calls=%async_computation.14 | async-start | bytes 5242880
  28.2 229.9 %copy-start.7 = (bf16[16,2,16,256]{3,2,0,1:T(8,128)(2,1)}, bf16[16,2,16,256]{3,2,0,1:T(8,128)(2,1)S(1)}, u32[]{:S(2)}) copy-start(bf16[16,2,16,256]{3,2,0,1:T(8,128)(2,1)S(1)} %all_gather.26) | copy-start | bytes 786436
  30.0 152.9 %copy-start.23 = (f32[256,16]{0,1:T(8,128)}, f32[256,16]{0,1:T(8,128)S(1)}, u32[]{:S(2)}) copy-start(f32[256,16]{0,1:T(8,128)S(1)} %get-tuple-element.65) | copy-start | bytes 49156
  45.9 162.8 %copy-start.11 = (bf16[16,16,1024]{2,1,0:T(8,128)(2,1)}, bf16[16,16,1024]{2,1,0:T(8,128)(2,1)S(1)}, u32[]{:S(2)}) copy-start(bf16[16,16,1024]{2,1,0:T(8,128)(2,1)S(1)} %all_gather.27) | copy-start | bytes 1572868
  61.0 160.3 %copy-start.13 = (bf16[16,16,1024]{2,1,0:T(8,128)(2,1)}, bf16[16,16,1024]{2,1,0:T(8,128)(2,1)S(1)}, u32[]{:S(2)}) copy-start(bf16[16,16,1024]{2,1,0:T(8,128)(2,1)S(1)} %all_gather.28) | copy-start | bytes 1572868
  207.7 2.3 copy-start.19
  234.6 6.2 %copy-start.14 = (f32[256,2,64]{0,2,1:T(8,128)S(1)}, f32[256,2,64]{0,2,1:T(8,128)}, u32[]{:S(2)}) copy-start(f32[256,2,64]{0,2,1:T(8,128)} %get-tuple-element.50) | copy-start | bytes 393220
  234.6 6.1 copy-start.15
  240.9 4.2 copy-start.20
  245.1 4.5 copy-start.29
  245.1 2.3 copy-start.18
  245.1 2.3 copy-start.28
  247.3 11.6 %copy-start.9 = (bf16[2,128,256]{2,1,0:T(8,128)(2,1)}, bf16[2,128,256]{2,1,0:T(8,128)(2,1)S(1)}, u32[]{:S(2)}) copy-start(bf16[2,128,256]{2,1,0:T(8,128)(2,1)S(1)} %fusion.28) | copy-start | bytes 393220
  247.4 2.2 copy-start.16
  247.7 12.3 %copy-start.2 = (bf16[2,128,4,256]{3,1,2,0:T(8,128)(2,1)}, bf16[2,128,4,256]{3,1,2,0:T(8,128)(2,1)S(1)}, u32[]{:S(2)}) copy-start(bf16[2,128,4,256]{3,1,2,0:T(8,128)(2,1)S(1)} %convolution_convert_fusion) | copy-start | bytes 1572868
  249.5 4.3 copy-start.21
  253.8 4.3 copy-start.24
  258.9 2.5 copy-start.8
  262.7 1.5 copy-start.12
  262.7 1.5 copy-start.25
  264.0 0.7 copy-start.26
  264.2 16.6 %copy-start.4 = (bf16[256,2,4,128]{0,3,2,1:T(8,128)(2,1)}, bf16[256,2,4,128]{0,3,2,1:T(8,128)(2,1)S(1)}, u32[]{:S(2)}) copy-start(bf16[256,2,4,128]{0,3,2,1:T(8,128)(2,1)S(1)} %fusion.44) | copy-start | bytes 1572868
  285.5 4.5 copy-start.5
  285.5 4.5 copy-start.17
  287.5 4.1 copy-start.6
  287.5 103.1 %reduce-scatter.17.cloned.1.call-start = ((), (), s32[]{:S(2)}) async-start(), calls=%async_computation.13 | async-start | bytes 1179648 | tf_op jit(solution)/shard_map/reduce_scatter | solution.py:328
  290.0 134.1 %reduce-scatter.15.cloned.1.call-start = ((), (), s32[]{:S(2)}) async-start(), calls=%async_computation.12 | async-start | bytes 1179648 | tf_op jit(solution)/shard_map/reduce_scatter | solution.py:326
  291.5 1.4 copy-start.3
  291.5 187.2 %reduce-scatter.9.cloned.1.call-start = ((), (), s32[]{:S(2)}) async-start(), calls=%async_computation.8 | async-start | bytes 5242880 | tf_op jit(solution)/shard_map/reduce_scatter | solution.py:223
  305.2 1.2 copy-start
  305.3 229.9 %reduce-scatter.11.cloned.1.call-start = ((), (), s32[]{:S(2)}) async-start(), calls=%async_computation.10 | async-start | bytes 5242880 | tf_op jit(solution)/shard_map/reduce_scatter | solution.py:321
  326.1 6.4 %copy-start.10 = (bf16[2,128,256]{2,1,0:T(8,128)(2,1)S(1)}, bf16[2,128,256]{2,1,0:T(8,128)(2,1)}, u32[]{:S(2)}) copy-start(bf16[2,128,256]{2,1,0:T(8,128)(2,1)} %copy-done.9) | copy-start | bytes 393220
  332.5 3.9 copy-start.1
  340.1 267.7 %reduce-scatter.13.cloned.1.call-start = ((), (), s32[]{:S(2)}) async-start(), calls=%async_computation.11 | async-start | bytes 7077888 | tf_op jit(solution)/shard_map/reduce_scatter | solution.py:325
  345.0 0.7 copy-start.27
Sparse Core Ops, SparseCore 0:
  9.6 25.4 all-gather.9
  37.0 52.5 all-gather.11
  91.2 38.2 all-gather.7
  131.2 51.5 all-gather.5
  287.6 68.8 all-reduce.5
  359.2 31.3 reduce-scatter.16
  393.4 30.5 reduce-scatter.14
  427.6 51.0 reduce-scatter.8
  482.5 52.6 reduce-scatter.10
  537.9 69.7 reduce-scatter.12
where the time goes:
time: 622 us; the launch traced here: 615 us
  waiting for transfers between devices  370 us (59%)
  matrix products  117 us (19%)
  blocking collectives  86.6 us (14%)
  between operations  15.6 us (3%)
  local copies, waits for them, and re-layouts  12.6 us (2%)
  other arithmetic  12 us (2%)
    reduce_scatter x1, waiting for transfers between devices, local(): lax.psum_scatter(input_down_gradient, 'dp', scatter_dimension=0, tiled=True)  72.6 us
    reduce_scatter x1, waiting for transfers between devices, local(): lax.psum_scatter((heads_sum + placed).astype(jnp.bfloat16), 'tensor', sca...  56.5 us
    reduce_scatter x1, waiting for transfers between devices, local(): lax.psum_scatter((jnp.dot(blended_output, output_weight, preferred_elemen...  54.6 us
    all_gather x1, waiting for transfers between devices, local(): gathered = lax.all_gather(hidden_in, 'tensor', axis=0, tiled=True)  53.3 us
    dot_general x10, matrix products, contract_trailing_axis(): lax.dot_general(left, right, (((1,), (1,)), ((), ())), preferred_element_...  51.3 us
    reduce_scatter x1, waiting for transfers between devices, local(): lax.psum_scatter(query_up_gradient, 'dp', scatter_dimension=0, tiled=True)  33.5 us
    reduce_scatter x1, waiting for transfers between devices, local(): lax.psum_scatter(output_down_gradient, 'dp', scatter_dimension=0, tiled=T...  30.9 us
    all_gather x1, waiting for transfers between devices, local(): incoming_gradient = lax.all_gather(out_grad, 'tensor', axis=0, tiled=True)  28.5 us
  transfers between devices with their start and end apart: 10, of which 9 were waited for; matrix products, arithmetic and copies ran while one was open for 11% of the time, Pallas kernels for 0%

commit v1 on v0

--- a/solution.py
+++ b/solution.py
@@ -164,7 +164,14 @@
         adapter_overall_count * adapter_rank_rows, query_columns
     )
     output_up_flattened = b_out_all.reshape(adapter_overall_count * rank_piece, full_width)
-    gathered = lax.all_gather(hidden_in, "tensor", axis=0, tiled=True)
+    ring = [hidden_in]
+    for hop in range(3):
+        ring.append(lax.ppermute(ring[-1], "tensor", [(dev, (dev + 1) % 4) for dev in range(4)]))
+    gathered = jnp.roll(
+        jnp.concatenate(ring[::-1], axis=0),
+        (lax.axis_index("tensor") + 1) * ring[0].shape[0],
+        axis=0,
+    )
     col_start = own_slot * narrow_cast
     local_columns = lax.dynamic_slice_in_dim(gathered, col_start, narrow_cast, 1)
     rank_partial_sum = choose_rank_rows(

time: 622 us -> 568 us (0.913)
  waiting for transfers between devices: 370 us -> 303 us
  local copies, waits for them, and re-layouts: 12.6 us -> 22.2 us
    all_gather x1 -> x0, waiting for transfers between devices: 53.3 us -> none  [local(): gathered = lax.all_gather(hidden_in, 'tensor', axis=0, tiled=True)]
    ppermute x0 -> x3, waiting for transfers between devices: none -> 44.2 us  [local(): lax.ppermute(ring[-1], 'tensor', [(dev, (dev + 1) % 4) for dev in range(4)])]
    all_gather x1, waiting for transfers between devices: 28.5 us -> 0.01 us  [local(): incoming_gradient = lax.all_gather(out_grad, 'tensor', axis=0, tiled=True)]
    all_gather x1, waiting for transfers between devices: 28 us -> 0.01 us  [local(): lax.all_gather(a_in, 'dp', axis=0, tiled=True)]
    unnamed x66 -> x75, local copies, waits for them, and re-layouts: 7.41 us -> 15.5 us
  transfers between devices with their start and end apart: 10 -> 12, of which waited for: 9 -> 8; matrix products, arithmetic and copies ran while one was open for 11% -> 19% of each run, Pallas kernels for 0% -> 0%
where the time goes in v1:
time: 568 us; the launch traced here: 563 us
  waiting for transfers between devices  303 us (53%)
  matrix products  112 us (20%)
  blocking collectives  90.4 us (16%)
  local copies, waits for them, and re-layouts  22.2 us (4%)
  other arithmetic  15.6 us (3%)
  between operations  15.3 us (3%)
    reduce_scatter x1, waiting for transfers between devices, local(): lax.psum_scatter(input_down_gradient, 'dp', scatter_dimension=0, tiled=True)  72.7 us
    reduce_scatter x1, waiting for transfers between devices, local(): lax.psum_scatter((jnp.dot(blended_output, output_weight, preferred_elemen...  56.5 us
    reduce_scatter x1, waiting for transfers between devices, local(): lax.psum_scatter((heads_sum + placed).astype(jnp.bfloat16), 'tensor', sca...  54.5 us
    dot_general x10, matrix products, contract_trailing_axis(): lax.dot_general(left, right, (((1,), (1,)), ((), ())), preferred_element_...  49.5 us
    ppermute x3, waiting for transfers between devices, local(): lax.ppermute(ring[-1], 'tensor', [(dev, (dev + 1) % 4) for dev in range(4)])  44.2 us
    reduce_scatter x1, waiting for transfers between devices, local(): lax.psum_scatter(output_down_gradient, 'dp', scatter_dimension=0, tiled=T...  33.3 us
    reduce_scatter x1, waiting for transfers between devices, local(): lax.psum_scatter(query_up_gradient, 'dp', scatter_dimension=0, tiled=True)  31 us
    psum x1, blocking collectives, local(): input_rank_rows = lax.psum(rank_partial_sum, 'tensor').astype(jnp.bfloat16)  17.6 us
  transfers between devices with their start and end apart: 12, of which 8 were waited for; matrix products, arithmetic and copies ran while one was open for 19% of the time, Pallas kernels for 0%

profile of v1, /device:TPU:0, one launch (start us, length us, event | category | flops | bytes accessed | tf_op | source)
XLA Modules:
  0.0 563.2 jit_solution(10472017721847437935)
XLA Ops:
  8.7 3.0 collective-permute-start
  11.8 24.3 %collective-permute-done = bf16[64,8192]{1,0:T(8,128)(2,1)S(1)} collective-permute-done((bf16[64,8192]{1,0:T(8,128)(2,1)}, bf16[64,8192]{1,0:T(8,128)(2,1)S(1)}, u32[]{:S(2)}, u32[]{:S(2)}) %collective-permute-start) | collective-permute-done | bytes 1048608 | tf_op jit(solution)/shard_map/ppermute | solution.py:169
  36.0 0.8 collective-permute-start.1
  37.6 0.8 reduce-window.4
  40.4 1.0 multiply_cosine_fusion
  41.4 20.0 %collective-permute-done.1 = bf16[64,8192]{1,0:T(8,128)(2,1)S(1)} collective-permute-done((bf16[64,8192]{1,0:T(8,128)(2,1)S(1)}, bf16[64,8192]{1,0:T(8,128)(2,1)S(1)}, u32[]{:S(2)}, u32[]{:S(2)}) %collective-permute-start.1) | collective-permute-done | bytes 1048608 | tf_op jit(solution)/shard_map/ppermute | solution.py:169
  61.4 15.9 %all_gather.22 = bf16[16,2,16,256]{3,2,0,1:T(8,128)(2,1)} all-gather(bf16[2,2,16,256]{3,2,0,1:T(8,128)(2,1)S(1)} %copy.119), channel_id=1, replica_groups=mesh['dp'=8,'tensor'=4] {'dp'}, dimensions={0}, use_global_device_ids=true | all-gather | bytes 294912 | tf_op jit(solution)/shard_map/all_gather | solution.py:140
  77.3 1.0 fusion.102
  79.1 16.0 %all_gather.23 = bf16[16,16,1024]{2,1,0:T(8,128)(2,1)} all-gather(bf16[2,16,1024]{2,1,0:T(8,128)(2,1)} %param.20), channel_id=1, replica_groups=mesh['dp'=8,'tensor'=4] {'dp'}, dimensions={0}, use_global_device_ids=true | all-gather | bytes 589824 | tf_op jit(solution)/shard_map/all_gather | solution.py:139
  95.1 16.0 %all_gather.24 = bf16[16,16,1024]{2,1,0:T(8,128)(2,1)} all-gather(bf16[2,16,1024]{2,1,0:T(8,128)(2,1)} %param.22), channel_id=1, replica_groups=mesh['dp'=8,'tensor'=4] {'dp'}, dimensions={0}, use_global_device_ids=true | all-gather | bytes 589824 | tf_op jit(solution)/shard_map/all_gather | solution.py:141
  111.1 1.7 fusion.117
  112.8 1.0 constant_dynamic-update-slice_fusion.7
  113.8 1.1 constant_dynamic-update-slice_fusion.6
  114.9 1.1 constant_dynamic-update-slice_fusion.5
  115.9 1.1 constant_dynamic-update-slice_fusion.4
  117.0 1.0 constant_dynamic-update-slice_fusion.3
  118.1 1.1 constant_dynamic-update-slice_fusion.2
  119.1 1.1 constant_dynamic-update-slice_fusion.1
  120.2 1.1 constant_dynamic-update-slice_fusion
  121.3 3.4 fusion.31
  124.7 17.6 %psum.21 = bf16[256,48]{0,1:T(8,128)(2,1)S(1)} all-reduce(f32[256,48]{0,1:T(8,128)S(1)} %fusion.31), channel_id=1, replica_groups=mesh['dp'=8,'tensor'=4] {'tensor'}, use_global_device_ids=true, to_apply=%region_3.4 | all-reduce | flops 12288 | bytes 73728 | tf_op jit(solution)/shard_map/psum | solution.py:182
  142.7 9.5 %fusion.26 = f32[256,1024]{1,0:T(8,128)S(1)} fusion(f32[256,1024]{1,0:T(8,128)S(1)} %fusion.29, bf16[8192,1024]{1,0:T(8,128)(2,1)} %param.16, bf16[512,8192]{1,0:T(8,128)(2,1)} %constant_dynamic-update-slice_fusion, s32[]{:T(128)S(6)} %select_n.29), kind=kOutput, calls=%fused_computation.37 | convolution fusion | flops 4295229440 | bytes 23068676 | tf_op jit(solution)/shard_map/dot_general | solution.py:190
  153.5 5.2 fusion.37
  159.6 2.2 fusion.119
  161.8 5.3 fusion.43
  167.5 0.8 copy-done.3
  168.3 0.9 fusion.48
  169.2 3.9 fusion.55
  173.1 8.4 %all-gather = bf16[4,4,256]{2,1,0:T(4,128)(2,1)S(1)} all-gather(bf16[1,4,256]{2,1,0:T(4,128)(2,1)S(1)} %fusion.104), channel_id=1, replica_groups=mesh['dp'=8,'tensor'=4] {'tensor'}, dimensions={0}, use_global_device_ids=true | all-gather | bytes 10240 | tf_op jit(solution)/shard_map/all_gather | solution.py:249
  181.8 11.6 %fusion.30 = bf16[256,1024]{1,0:T(8,128)(2,1)S(1)} fusion(f32[256,1024]{1,0:T(8,128)S(1)} %convolution_bitcast_fusion.2, bf16[256,8192]{1,0:T(8,128)(2,1)} %all-gather.9.cloned.1.call-done, bf16[1024,8192]{1,0:T(8,128)(2,1)} %param.18), kind=kOutput, calls=%fused_computation.44 | convolution fusion | flops 4295491584 | bytes 22544384 | tf_op jit(solution)/shard_map/dot_general | solution.py:13
  194.1 2.8 fusion.42
  196.9 3.7 convolution_bitcast_fusion.5
  200.6 3.0 fusion.70
  203.6 1.0 slice_negate_fusion.2
  204.6 1.0 fusion.82
  205.7 1.1 convolution_multiply_fusion.4
  206.8 0.8 copy.139
  207.6 1.2 convolution_multiply_fusion.3
  208.8 0.8 copy.141
  209.8 1.2 broadcast_multiply_fusion
  212.3 16.6 %all-reduce.3 = (bf16[256,16]{0,1:T(8,128)(2,1)S(1)}, f32[256,48]{0,1:T(8,128)}) all-reduce(f32[256,16]{0,1:T(8,128)S(1)} %copy-done.27, f32[256,48]{0,1:T(8,128)S(1)} %pad_maximum_fusion.4), channel_id=1, replica_groups=mesh['dp'=8,'tensor'=4] {'tensor'}, use_global_device_ids=true, to_apply=%region_9.10 | all-reduce | flops 16384 | bytes 122880 | tf_op jit(solution)/shard_map/psum | solution.py:224
  229.5 3.0 convolution_multiply_fusion
  232.6 1.7 reshape.308
  234.3 2.0 pad_maximum_fusion.1
  236.3 2.4 convolution_multiply_fusion.1
  239.2 0.8 multiply_convert_fusion
  240.0 1.3 fusion.91
  241.3 19.1 %fusion.121 = f32[256,8192]{1,0:T(8,128)} fusion(bf16[256,1024]{0,1:T(8,128)(2,1)S(1)} %fusion.61, bf16[8192,1024]{1,0:T(8,128)(2,1)} %param.16), kind=kOutput, calls=%fused_computation.175 | convolution fusion | flops 4294967296 | bytes 25690112 | tf_op jit(solution)/shard_map/dot_general | solution.py:13
  260.4 6.1 %convolution_add_fusion.1 = f32[256,8192]{1,0:T(8,128)S(1)} fusion(f32[256,8192]{1,0:T(8,128)} %fusion.121, bf16[256,256]{0,1:T(8,128)(2,1)S(1)} %bitcast.245, bf16[2,8192,256]{2,1,0:T(8,128)(2,1)} %param.17), kind=kOutput, calls=%fused_computation.3 | convolution fusion | flops 1075838976 | bytes 21102592 | tf_op jit(solution)/shard_map/dot_general | solution.py:13
  266.6 3.8 convolution_add_fusion
  270.4 1.2 fusion.21
  271.6 2.5 convert_element_type.128
  274.4 0.9 copy-done.8
  275.4 1.3 fusion.2
  276.7 12.6 %fusion.3 = bf16[256,8192]{1,0:T(8,128)(2,1)} fusion(f32[256,8192]{1,0:T(8,128)S(1)} %fusion.2, bf16[256,1024]{0,1:T(8,128)(2,1)S(1)} %bitcast.236, bf16[1024,8192]{1,0:T(8,128)(2,1)} %param.18), kind=kOutput, calls=%fused_computation.7 | convolution fusion | flops 4299161600 | bytes 29884416 | tf_op jit(solution)/shard_map/dot_general | solution.py:232
  289.4 5.1 fusion.64
  296.4 8.8 %all-reduce.6.cloned.1.call-done = (f32[16,2,16,256]{3,2,0,1:T(8,128)}, f32[16,4,8192]{2,1,0:T(4,128)}) async-done(((f32[16,2,16,256]{3,2,0,1:T(8,128)}, f32[16,4,8192]{2,1,0:T(4,128)}), (f32[16,2,16,256]{3,2,0,1:T(8,128)}, f32[16,4,8192]{2,1,0:T(4,128)})) %all-reduce.6.cloned.1.call-update) | async-done | bytes 2621456
  305.2 0.8 constant_dynamic-slice_fusion.1
  306.7 1.7 constant_dynamic-slice_fusion
  308.4 31.0 %reduce-scatter.15.cloned.1.call-done = f32[2,16,1024]{2,1,0:T(8,128)} async-done(((f32[16,16,1024]{2,1,0:T(8,128)}), f32[2,16,1024]{2,1,0:T(8,128)}) %reduce-scatter.15.cloned.1.call-update) | async-done | bytes 131088 | tf_op jit(solution)/shard_map/reduce_scatter | solution.py:333
  339.3 33.3 %reduce-scatter.17.cloned.1.call-done = f32[2,16,1024]{2,1,0:T(8,128)} async-done(((f32[16,16,1024]{2,1,0:T(8,128)}), f32[2,16,1024]{2,1,0:T(8,128)}) %reduce-scatter.17.cloned.1.call-update) | async-done | bytes 131088 | tf_op jit(solution)/shard_map/reduce_scatter | solution.py:335
  372.7 54.5 %reduce-scatter.11.cloned.1.call-done = bf16[64,8192]{1,0:T(8,128)(2,1)} async-done(((bf16[256,8192]{1,0:T(8,128)(2,1)}), bf16[64,8192]{1,0:T(8,128)(2,1)}) %reduce-scatter.11.cloned.1.call-update) | async-done | bytes 1048592 | tf_op jit(solution)/shard_map/reduce_scatter | solution.py:328
  427.2 56.5 %reduce-scatter.9.cloned.1.call-done = bf16[64,8192]{1,0:T(8,128)(2,1)} async-done(((bf16[256,8192]{1,0:T(8,128)(2,1)}), bf16[64,8192]{1,0:T(8,128)(2,1)}) %reduce-scatter.9.cloned.1.call-update) | async-done | bytes 1048592 | tf_op jit(solution)/shard_map/reduce_scatter | solution.py:230
  483.7 72.7 %reduce-scatter.13.cloned.1.call-done = f32[2,48,2048]{2,1,0:T(8,128)} async-done(((f32[16,48,2048]{2,1,0:T(8,128)}), f32[2,48,2048]{2,1,0:T(8,128)}) %reduce-scatter.13.cloned.1.call-update) | async-done | bytes 786448 | tf_op jit(solution)/shard_map/reduce_scatter | solution.py:332
  (118 shorter events, 13.6 us)
Async XLA Ops:
  7.2 114.1 %all-gather.5.cloned.1.call-start = ((), (), s32[]{:S(2)}) async-start(), calls=%async_computation.5 | async-start | bytes 3538944 | tf_op jit(solution)/shard_map/all_gather | solution.py:138
  7.9 161.3 %all-gather.7.cloned.1.call-start = ((), (), s32[]{:S(2)}) async-start(), calls=%async_computation.6 | async-start | bytes 1179648 | tf_op jit(solution)/shard_map/all_gather | solution.py:142
  8.6 160.5 %all-gather.9.cloned.1.call-start = ((), (), s32[]{:S(2)}) async-start(), calls=%async_computation.8 | async-start | bytes 5242880 | tf_op jit(solution)/shard_map/all_gather | solution.py:240
  8.7 27.3 %collective-permute-start = (bf16[64,8192]{1,0:T(8,128)(2,1)}, bf16[64,8192]{1,0:T(8,128)(2,1)S(1)}, u32[]{:S(2)}, u32[]{:S(2)}) collective-permute-start(bf16[64,8192]{1,0:T(8,128)(2,1)} %param.12), channel_id=1, source_target_pairs={{0,1},{1,2},{2,3},{3,0},{4,5},{5,6},{6,7},{7,4},{8,9},{9,10},{10,1... | collective-permute-start | bytes 3145736 | tf_op jit(solution)/shard_map/ppermute | solution.py:169
  11.7 293.5 %all-reduce.6.cloned.1.call-start = ((), (), s32[]{:S(2)}) async-start(), calls=%async_computation.13 | async-start | bytes 5242880
  36.0 25.4 %collective-permute-start.1 = (bf16[64,8192]{1,0:T(8,128)(2,1)S(1)}, bf16[64,8192]{1,0:T(8,128)(2,1)S(1)}, u32[]{:S(2)}, u32[]{:S(2)}) collective-permute-start(bf16[64,8192]{1,0:T(8,128)(2,1)S(1)} %collective-permute-done), channel_id=1, source_target_pairs={{0,1},{1,2},{2,3},{3,0},{4,5},{5,6},{6,7},{7,4},{8,9},{9,10},{10,1... | collective-permute-start | bytes 3145736 | tf_op jit(solution)/shard_map/ppermute | solution.py:169
  61.4 51.4 %collective-permute-start.2 = (bf16[64,8192]{1,0:T(8,128)(2,1)S(1)}, bf16[64,8192]{1,0:T(8,128)(2,1)S(1)}, u32[]{:S(2)}, u32[]{:S(2)}) collective-permute-start(bf16[64,8192]{1,0:T(8,128)(2,1)S(1)} %collective-permute-done.1), channel_id=1, source_target_pairs={{0,1},{1,2},{2,3},{3,0},{4,5},{5,6},{6,7},{7,4},{8,9},{9,10},{10,1... | collective-permute-start | bytes 3145736 | tf_op jit(solution)/shard_map/ppermute | solution.py:169
  77.3 38.7 %copy-start.1 = (bf16[64,8192]{1,0:T(8,128)(2,1)S(1)}, bf16[64,8192]{1,0:T(8,128)(2,1)}, u32[]{:S(2)}) copy-start(bf16[64,8192]{1,0:T(8,128)(2,1)} %param.12) | copy-start | bytes 3145732
  118.1 3.2 copy-start.25
  121.3 21.1 %copy-start.12 = (bf16[16,16,1024]{2,1,0:T(8,128)(2,1)S(1)}, bf16[16,16,1024]{2,1,0:T(8,128)(2,1)}, u32[]{:S(2)}) copy-start(bf16[16,16,1024]{2,1,0:T(8,128)(2,1)} %all_gather.23) | copy-start | bytes 1572868
  142.7 10.5 %copy-start.18 = (bf16[16,1,16,256]{3,2,0,1:T(8,128)(2,1)S(1)}, bf16[16,1,16,256]{3,2,0,1:T(8,128)(2,1)}, u32[]{:S(2)}) copy-start(bf16[16,1,16,256]{3,2,0,1:T(8,128)(2,1)} %get-tuple-element.52) | copy-start | bytes 393220
  153.2 5.5 copy-start.7
  153.2 5.5 copy-start.6
  153.5 5.3 copy-start.17
  158.7 0.8 copy-start.24
  159.1 2.6 copy-start.22
  159.6 7.5 %copy-start.15 = (bf16[256,2,4,128]{0,3,2,1:T(8,128)(2,1)}, bf16[256,2,4,128]{0,3,2,1:T(8,128)(2,1)S(1)}, u32[]{:S(2)}) copy-start(bf16[256,2,4,128]{0,3,2,1:T(8,128)(2,1)S(1)} %fusion.59) | copy-start | bytes 1572868
  161.7 5.4 copy-start.30
  161.7 5.4 copy-start.29
  167.1 1.2 copy-start.14
  167.5 0.8 copy-start.3
  194.1 2.8 copy-start.16
  196.9 3.7 copy-start.23
  209.7 1.5 copy-start.13
  209.7 1.5 copy-start.26
  210.9 0.9 copy-start.9
  210.9 1.2 copy-start.10
  211.0 1.4 copy-start.27
  211.2 17.8 %copy-start.5 = (bf16[256,2,4,128]{0,3,2,1:T(8,128)(2,1)}, bf16[256,2,4,128]{0,3,2,1:T(8,128)(2,1)S(1)}, u32[]{:S(2)}) copy-start(bf16[256,2,4,128]{0,3,2,1:T(8,128)(2,1)S(1)} %fusion.63) | copy-start | bytes 1572868
  228.9 0.6 copy-start.20
  232.6 3.7 copy-start.19
  234.3 4.7 copy-start
  236.2 3.7 copy-start.4
  236.3 103.1 %reduce-scatter.15.cloned.1.call-start = ((), (), s32[]{:S(2)}) async-start(), calls=%async_computation.11 | async-start | bytes 1179648 | tf_op jit(solution)/shard_map/reduce_scatter | solution.py:333
  238.8 133.9 %reduce-scatter.17.cloned.1.call-start = ((), (), s32[]{:S(2)}) async-start(), calls=%async_computation.12 | async-start | bytes 1179648 | tf_op jit(solution)/shard_map/reduce_scatter | solution.py:335
  260.4 6.2 %copy-start.11 = (bf16[2,128,256]{2,1,0:T(8,128)(2,1)S(1)}, bf16[2,128,256]{2,1,0:T(8,128)(2,1)}, u32[]{:S(2)}) copy-start(bf16[2,128,256]{2,1,0:T(8,128)(2,1)} %fusion.42) | copy-start | bytes 393220
  260.4 166.8 %reduce-scatter.11.cloned.1.call-start = ((), (), s32[]{:S(2)}) async-start(), calls=%async_computation.9 | async-start | bytes 5242880 | tf_op jit(solution)/shard_map/reduce_scatter | solution.py:328
  266.6 3.9 copy-start.2
  274.1 1.2 copy-start.8
  274.2 1.2 copy-start.21
  274.2 209.5 %reduce-scatter.9.cloned.1.call-start = ((), (), s32[]{:S(2)}) async-start(), calls=%async_computation.7 | async-start | bytes 5242880 | tf_op jit(solution)/shard_map/reduce_scatter | solution.py:230
  289.3 267.1 %reduce-scatter.13.cloned.1.call-start = ((), (), s32[]{:S(2)}) async-start(), calls=%async_computation.10 | async-start | bytes 7077888 | tf_op jit(solution)/shard_map/reduce_scatter | solution.py:332
  294.5 0.7 copy-start.28
Sparse Core Ops, SparseCore 0:
  9.6 40.9 all-gather.4
  52.3 21.9 all-gather.6
  76.1 52.3 all-gather.8
  236.4 68.7 all-reduce.5
  307.9 31.3 reduce-scatter.14
  342.0 30.5 reduce-scatter.16
  376.2 50.9 reduce-scatter.10
  431.0 52.6 reduce-scatter.8
  486.6 69.7 reduce-scatter.12
